TPU v7x, 32 devices: a whole 2x2x4 slice. The times are simulated.
32 devices in a mesh: dp: 4 (over x, core), ref: 8 (over z, y).
Axes of the slice: x: 2, y: 2, z: 4, core: 2. Of those that a mesh axis runs over, the one named last changes fastest.
Arguments:
- candidates: float32 [384, 64], P('ref'), may hold values from -6 to 6
- observed: float32 [8192, 64], P('dp'), may hold values from -6 to 6
- ref_points: float32 [8192, 64], P('ref'), may hold values from -6 to 6
- slab: float32 [8192, 8192], P('dp', 'ref'), may hold values from -0.3125 to 0.3125
- ref_weight: float32 [8192], P('ref'), may hold values from 0.2 to 2
- inv_scale: float32 [64], replicated, may hold values from 0.06 to 0.2
Outputs:
- ascent: float32 [384, 64], P('ref')
- value: float32 [384], P('ref')
All inputs are finite; a program needn't handle non-finite values.
Results may differ from a plain program's by a relative error of at most 0.000067.
Values sent between devices are 32-bit elements; how exact they have to be, the bound alone decides.
A program may use at most 64 MiB of HBM per device.

v0:
```python
import functools

import jax
import jax.numpy as jnp
from jax import lax
from jax.experimental import pallas as pl
from jax.experimental.pallas import tpu as pltpu
from jax.sharding import PartitionSpec as P

F32, BF16 = jnp.float32, jnp.bfloat16
MESH = pl.DeviceIdType.MESH
CHUNK = 256
BLOCK = 256
ROWS = 1024
NT = (((1,), (1,)), ((), ()))
VMEM_BYTES = 60 * 1024 * 1024


def split(x):
    hi = x.astype(BF16)
    return hi, (x - hi.astype(F32)).astype(BF16)


def half_rows(own):
    return -(-own // 16) * 8


def mm(a, b):
    return jnp.dot(a, b, preferred_element_type=F32)


def mm_nt(a, b):
    return lax.dot_general(a, b, NT, preferred_element_type=F32)


def two_halves(x):
    hi = x.astype(BF16).astype(F32)
    return jnp.concatenate([hi, x - hi], axis=0).astype(BF16)


def kernel(n_dp, n_ref,
           cand_ref, obs_ref, refp_ref, slab_ref, rw_ref, inv_ref,
           packed_ref,
           stage, s2, k2, kf, kt, kref, bmat, vnorm, o2, amat, unorm, cand_all,
           pbuf, a_recv, b_buf, b_recv, w_buf, w_recv, acc,
           gout, r_recv, d_send_buf, d_recv_buf, gt, dgrad, dloss,
           slab_sem, g_ss, g_rs, a_ss, a_rs, b_ss, b_rs, c_ss, c_rs, r_ss, r_rs, d_ss, d_rs):
    dp, rf = lax.axis_index("dp"), lax.axis_index("ref")
    core, xi = lax.rem(dp, 2), dp // 2
    other = 1 - core
    partner = xi * 2 + other
    nx = n_dp // 2
    own, feat = cand_ref.shape
    q = own * n_ref
    half = q // 2
    obs_n, ref_n = slab_ref.shape
    nj = ref_n // CHUNK
    left = half_rows(own)

    def peer_ref(k):
        return (dp, lax.rem(rf + k, n_ref))

    def peer_dp(k):
        return (lax.rem(dp + k, n_dp), rf)

    def slab_copy(j):
        return pltpu.make_async_copy(
            slab_ref.at[:, pl.ds(pl.multiple_of(j * CHUNK, CHUNK), CHUNK)], stage.at[j], slab_sem.at[j])

    for j in range(nj):
        slab_copy(j).start()
    barrier = pltpu.get_barrier_semaphore()
    for k in range(1, n_ref):
        pl.semaphore_signal(barrier, inc=1, device_id=peer_ref(k), device_id_type=MESH)
    for k in range(1, n_dp):
        pl.semaphore_signal(barrier, inc=1, device_id=peer_dp(k), device_id_type=MESH)

    inv = inv_ref[...]
    inv_col = jnp.broadcast_to(inv, (8, feat)).T[:, 0:1]

    def prep(src, base, n):
        @pl.loop(0, n // BLOCK)
        def _(i):
            cols = pl.ds(pl.multiple_of(i * BLOCK, BLOCK), BLOCK)
            to = pl.ds(pl.multiple_of(base + i * BLOCK, BLOCK), BLOCK)
            v = src[:, cols]
            o2[0:2 * feat, to] = two_halves(v)
            o2[2 * feat:2 * feat + 16, to] = jnp.ones((16, BLOCK), BF16)
            sc = v * inv_col
            b1 = two_halves(sc)
            bmat[0:2 * feat, to] = b1
            bmat[2 * feat:4 * feat, to] = b1
            vnorm[:, to] = jnp.sum(sc * sc, axis=0, keepdims=True)

    prep(obs_ref, 0, obs_n)

    def split_slab(j):
        @pl.loop(0, obs_n // BLOCK)
        def _(i):
            rows = pl.ds(pl.multiple_of(i * BLOCK, BLOCK), BLOCK)
            hi, lo = split(stage[j, rows, :])
            s2[j, rows, 0:CHUNK] = hi
            s2[j, rows, CHUNK:2 * CHUNK] = lo

    pl.semaphore_wait(barrier, n_ref - 1 + n_dp - 1)

    def gather(k):
        return pltpu.make_async_remote_copy(
            src_ref=cand_ref, dst_ref=cand_all.at[rf], send_sem=g_ss.at[k], recv_sem=g_rs.at[k],
            device_id=peer_ref(k), device_id_type=MESH)

    for k in range(1, n_ref):
        gather(k).start()
    cand_all[rf] = cand_ref[...]

    prep(refp_ref, obs_n, ref_n)

    @pl.loop(0, nj)
    def _(j):
        slab_copy(j).wait()
        split_slab(j)

    for k in range(1, n_ref):
        gather(k).wait()

    u = cand_all[...].reshape(q, feat) * inv
    unorm[...] = jnp.sum(u * u, axis=1, keepdims=True)
    hi, lo = split(jnp.concatenate([u, u], axis=1))
    amat[:, 0:2 * feat] = hi
    amat[:, 2 * feat:4 * feat] = lo

    def kvals(start):
        rows = pl.ds(pl.multiple_of(start, BLOCK), BLOCK)
        cross = mm(amat[...], bmat[:, rows])
        return jnp.exp(-0.5 * (unorm[...] + vnorm[:, rows] - 2.0 * cross))

    @pl.loop(0, obs_n // BLOCK)
    def _(i):
        cols = pl.ds(pl.multiple_of(i * BLOCK, BLOCK), BLOCK)
        kk = kvals(i * BLOCK)
        kf[:, cols] = kk
        khi, klo = split(kk)
        k2[:, 0:half, cols] = khi.reshape(2, half, BLOCK)
        k2[:, half:q, cols] = klo.reshape(2, half, BLOCK)

    def a_copy(j):
        return pltpu.make_async_remote_copy(
            src_ref=pbuf.at[j, other], dst_ref=a_recv.at[j], send_sem=a_ss.at[j], recv_sem=a_rs.at[j],
            device_id=(partner, rf), device_id_type=MESH)

    def b_copy(j, m):
        return pltpu.make_async_remote_copy(
            src_ref=b_buf.at[j], dst_ref=b_recv.at[j, m - 1], send_sem=b_ss.at[j, m], recv_sem=b_rs.at[j, m],
            device_id=(lax.rem(xi + m, nx) * 2 + core, rf), device_id_type=MESH)

    def c_copy(j):
        return pltpu.make_async_remote_copy(
            src_ref=w_buf.at[j], dst_ref=w_recv.at[j], send_sem=c_ss.at[j], recv_sem=c_rs.at[j],
            device_id=(partner, rf), device_id_type=MESH)

    def finish_a(j):
        a_copy(j).wait()
        b_buf[j] = pbuf[j, core] + a_recv[j]
        for m in range(1, nx):
            b_copy(j, m).start()

    def first(j, h):
        x = mm(k2[h], s2[j, :, 0:CHUNK])
        pbuf[j, h] = x[0:half] + x[half:q] + mm(k2[h, 0:half, :], s2[j, :, CHUNK:2 * CHUNK])

    @pl.loop(0, nj)
    def _(j):
        first(j, other)
        a_copy(j).start()

        @pl.when(j > 0)
        def _():
            finish_a(j - 1)

        first(j, core)

    finish_a(nj - 1)

    @pl.loop(0, ref_n // BLOCK)
    def _(i):
        cols = pl.ds(pl.multiple_of(i * BLOCK, BLOCK), BLOCK)
        kref[:, :, cols] = kvals(obs_n + i * BLOCK).reshape(2, half, BLOCK)

    @pl.loop(0, obs_n // BLOCK)
    def _(i):
        rows = pl.ds(pl.multiple_of(i * BLOCK, BLOCK), BLOCK)
        kt[rows, :] = kf[:, rows].T

    gt[...] = jnp.zeros_like(gt)
    gout[...] = jnp.zeros_like(gout)

    def second(j):
        c_copy(j).wait()
        w, wr = w_buf[j], w_recv[j]
        low = core == 0
        wt = jnp.concatenate([jnp.where(low, w, wr), jnp.where(low, wr, w)], axis=0).T
        whi, wlo = split(wt)
        whl = jnp.concatenate([whi, wlo], axis=1)

        @pl.loop(0, obs_n // ROWS)
        def _(i):
            rows = pl.ds(pl.multiple_of(i * ROWS, ROWS), ROWS)
            x = mm(s2[j, rows, 0:CHUNK], whl)
            prod = x[:, 0:q] + x[:, q:2 * q] + mm(s2[j, rows, CHUNK:2 * CHUNK], whi)
            if j > 0:
                prod = acc[rows, :] + prod
            if j < nj - 1:
                acc[rows, :] = prod
            else:
                back = -prod * kt[rows, :]
                bhi, blo = split(back)
                pts = o2[:, rows]
                gt[...] += mm(pts, bhi) + mm(pts, blo)

    for j in range(nj):
        cols = slice(j * CHUNK, (j + 1) * CHUNK)
        for m in range(1, nx):
            b_copy(j, m).wait()
        total = b_buf[j]
        for m in range(1, nx):
            total = total + b_recv[j, m - 1]
        kr = kref[core, :, cols]
        rw = rw_ref[0:1, cols]
        resid = kr - total
        w = 2.0 * rw * resid
        w_buf[j] = w
        c_copy(j).start()
        dhi, dlo = split(w * kr)
        pts = o2[:, obs_n + j * CHUNK:obs_n + (j + 1) * CHUNK]
        dg = mm_nt(dhi, pts) + mm_nt(dlo, pts)
        dl = rw * resid * resid
        if j == 0:
            dgrad[...], dloss[...] = dg, dl
        else:
            dgrad[...] += dg
            dloss[...] += dl
        if j > 0:
            second(j - 1)
    second(nj - 1)

    def combine(g, cands):
        return g[:, 0:feat] + g[:, feat:2 * feat] - cands * g[:, 2 * feat:2 * feat + 1]

    grad = combine(gt[...].T, cand_all[...].reshape(q, feat))
    hslots = n_ref // 2
    mask = (xi == 0).astype(F32)
    extra = combine(dgrad[...], cand_all[pl.ds(core * hslots, hslots)].reshape(half, feat)) * mask
    loss = jnp.sum(dloss[...].T, axis=0, keepdims=True) * mask
    rest = own - left
    for i in range(n_ref):
        at = i * own
        gout[i, 0:left, 0:feat] = grad[at:at + left]
        gout[i, 0:rest, feat:2 * feat] = grad[at + left:at + own]
    for i in range(hslots):
        at, slot = i * own, core * hslots + i
        gout[slot, 0:left, 0:feat] += extra[at:at + left]
        gout[slot, 0:rest, feat:2 * feat] += extra[at + left:at + own]
        gout[slot, left:left + 1, 0:own] = loss[:, at:at + own]

    def r_copy(k):
        return pltpu.make_async_remote_copy(
            src_ref=gout.at[lax.rem(rf + k, n_ref)], dst_ref=r_recv.at[k - 1],
            send_sem=r_ss.at[k], recv_sem=r_rs.at[k], device_id=peer_ref(k), device_id_type=MESH)

    def d_copy(k):
        return pltpu.make_async_remote_copy(
            src_ref=d_send_buf, dst_ref=d_recv_buf.at[k],
            send_sem=d_ss.at[k], recv_sem=d_rs.at[k], device_id=peer_dp(k), device_id_type=MESH)

    for k in range(1, n_ref):
        r_copy(k).start()
    total = gout[rf]
    for k in range(1, n_ref):
        r_copy(k).wait()
        total = total + r_recv[k - 1]
    d_send_buf[...] = total
    for k in range(1, n_dp):
        d_copy(k).start()
    d_recv_buf[0] = total
    for k in range(1, n_dp):
        d_copy(k).wait()
    result = d_recv_buf[dp]
    for i in range(1, n_dp):
        result = result + d_recv_buf[lax.rem(dp - i + n_dp, n_dp)]
    packed_ref[...] = result


def finish(refs_total, packed_ref, inv_ref, ascent_ref, value_ref):
    feat = inv_ref.shape[1]
    own = ascent_ref.shape[0]
    left = half_rows(own)
    inv = inv_ref[...]
    scale = 32.0 / jnp.sqrt(F32(refs_total)) * (inv * inv)
    ascent_ref[0:left, :] = scale * packed_ref[0:left, 0:feat]
    ascent_ref[left:own, :] = scale * packed_ref[0:own - left, feat:2 * feat]
    value_ref[...] = packed_ref[left:left + 1, 0:own] / refs_total


def body(candidates, observed, ref_points, slab, ref_weight, inv_scale):
    n_ref, n_dp = lax.axis_size("ref"), lax.axis_size("dp")
    own, feat = candidates.shape
    q = own * n_ref
    half = q // 2
    obs_n, ref_n = slab.shape
    nj, nx = ref_n // CHUNK, n_dp // 2
    rows = half_rows(own) + 8
    vm = pl.BlockSpec(memory_space=pltpu.VMEM)
    V = pltpu.VMEM
    dma = pltpu.SemaphoreType.DMA
    inv_row = inv_scale.reshape(1, feat)
    packed = pl.pallas_call(
        functools.partial(kernel, n_dp, n_ref),
        out_shape=jax.ShapeDtypeStruct((rows, 128), F32),
        in_specs=[vm, vm, vm, pl.BlockSpec(memory_space=pl.ANY), vm, vm],
        out_specs=vm,
        scratch_shapes=[
            V((nj, obs_n, CHUNK), F32), V((nj, obs_n, 2 * CHUNK), BF16),
            V((2, q, obs_n), BF16), V((q, obs_n), F32), V((obs_n, q), F32), V((2, half, ref_n), F32),
            V((4 * feat, obs_n + ref_n), BF16), V((1, obs_n + ref_n), F32), V((2 * feat + 16, obs_n + ref_n), BF16),
            V((q, 4 * feat), BF16), V((q, 1), F32), V((n_ref, own, feat), F32),
            V((nj, 2, half, CHUNK), F32), V((nj, half, CHUNK), F32), V((nj, half, CHUNK), F32),
            V((nj, max(nx - 1, 1), half, CHUNK), F32), V((nj, half, CHUNK), F32), V((nj, half, CHUNK), F32),
            V((obs_n, q), F32),
            V((n_ref, rows, 128), F32), V((n_ref - 1, rows, 128), F32), V((rows, 128), F32), V((n_dp, rows, 128), F32),
            V((2 * feat + 16, q), F32), V((half, 2 * feat + 16), F32), V((half, CHUNK), F32),
            dma((nj,)), dma((n_ref,)), dma((n_ref,)), dma((nj,)), dma((nj,)),
            dma((nj, nx)), dma((nj, nx)), dma((nj,)), dma((nj,)),
            dma((n_ref,)), dma((n_ref,)), dma((n_dp,)), dma((n_dp,)),
        ],
        compiler_params=pltpu.CompilerParams(
            collective_id=0, has_side_effects=True, vmem_limit_bytes=VMEM_BYTES),
        name="variance_grad",
    )(candidates, observed.T, ref_points.T, slab, ref_weight.reshape(1, ref_n), inv_row)
    ascent, value = pl.pallas_call(
        functools.partial(finish, ref_n * n_ref),
        out_shape=(jax.ShapeDtypeStruct((own, feat), F32), jax.ShapeDtypeStruct((1, own), F32)),
        in_specs=[vm, vm],
        out_specs=(vm, vm),
        name="scale_out",
    )(packed, inv_row)
    return ascent, value.reshape(own)


def solution(mesh):
    in_specs = (P("ref", None), P("dp", None), P("ref", None), P("dp", "ref"), P("ref"), P())
    out_specs = (P("ref", None), P("ref"))
    return jax.shard_map(body, mesh=mesh, in_specs=in_specs, out_specs=out_specs, check_vma=False)
```

profile of v0, /device:TPU:0, one launch (start us, length us, event | category | flops | bytes accessed | tf_op | source)
XLA Modules:
  0.0 53.4 jit_solution(16869308614749437599)
XLA Ops:
  0.6 51.3 %variance_grad.1.packed_ref = f32[32,128]{1,0:T(8,128)} custom-call(f32[48,64]{1,0:T(8,128)} %cand_ref.1, f32[64,2048]{1,0:T(8,128)} %bitcast.5, f32[64,1024]{1,0:T(8,128)} %bitcast.6, f32[2048,1024]{1,0:T(8,128)} %slab_ref.1, f32[1,1024]{1,0:T(1,128)} %bitcast.7, f32[1,64]{1,0:T(1,128)} %bitcast.8), custom_call_target="tpu_custom_call" | custom-call | tf_op jit(solution)/shard_map/variance_grad/pallas_call | solution.py:316
  52.0 1.4 %scale_out.1 = (f32[48,64]{1,0:T(8,128)}, f32[1,48]{1,0:T(1,128)}) custom-call(f32[32,128]{1,0:T(8,128)} %variance_grad.1.packed_ref, f32[1,64]{1,0:T(1,128)} %bitcast.9), custom_call_target="tpu_custom_call" | custom-call | tf_op jit(solution)/shard_map/scale_out/pallas_call | solution.py:339
where the time goes:
time: 53.6 us; the launch traced here: 53.4 us
  Pallas kernels  52.7 us (98%)
  between operations  0.64 us (1%)
    pallas_call x1, Pallas kernels, body(): pl.pallas_call(functools.partial(kernel, n_dp, n_ref), out_shape=jax.Shap...  51.3 us
    pallas_call x1, Pallas kernels, body(): pl.pallas_call(functools.partial(finish, ref_n * n_ref), out_shape=(jax.S...  1.4 us

commit v1 on v0

--- a/solution.py
+++ b/solution.py
@@ -39,11 +39,12 @@
 
 
 def kernel(n_dp, n_ref,
-           cand_ref, obs_ref, refp_ref, slab_ref, rw_ref, inv_ref,
+           cand_hbm, obs_hbm, refp_hbm, slab_ref, rw_hbm, inv_hbm,
            packed_ref,
            stage, s2, k2, kf, kt, kref, bmat, vnorm, o2, amat, unorm, cand_all,
            pbuf, a_recv, b_buf, b_recv, w_buf, w_recv, acc,
            gout, r_recv, d_send_buf, d_recv_buf, gt, dgrad, dloss,
+           cand_ref, obs_ref, refp_ref, rw_ref, inv_ref, in_sem,
            slab_sem, g_ss, g_rs, a_ss, a_rs, b_ss, b_rs, c_ss, c_rs, r_ss, r_rs, d_ss, d_rs):
     dp, rf = lax.axis_index("dp"), lax.axis_index("ref")
     core, xi = lax.rem(dp, 2), dp // 2
@@ -67,14 +68,20 @@
         return pltpu.make_async_copy(
             slab_ref.at[:, pl.ds(pl.multiple_of(j * CHUNK, CHUNK), CHUNK)], stage.at[j], slab_sem.at[j])
 
-    for j in range(nj):
-        slab_copy(j).start()
     barrier = pltpu.get_barrier_semaphore()
     for k in range(1, n_ref):
         pl.semaphore_signal(barrier, inc=1, device_id=peer_ref(k), device_id_type=MESH)
     for k in range(1, n_dp):
         pl.semaphore_signal(barrier, inc=1, device_id=peer_dp(k), device_id_type=MESH)
 
+    pairs = ((inv_hbm, inv_ref), (obs_hbm, obs_ref), (cand_hbm, cand_ref), (refp_hbm, refp_ref), (rw_hbm, rw_ref))
+    inputs = [pltpu.make_async_copy(src, dst, in_sem.at[i]) for i, (src, dst) in enumerate(pairs)]
+    for copy in inputs:
+        copy.start()
+    for j in range(nj):
+        slab_copy(j).start()
+    inputs[0].wait()
+    inputs[1].wait()
     inv = inv_ref[...]
     inv_col = jnp.broadcast_to(inv, (8, feat)).T[:, 0:1]
 
@@ -102,6 +109,8 @@
             s2[j, rows, 0:CHUNK] = hi
             s2[j, rows, CHUNK:2 * CHUNK] = lo
 
+    for copy in inputs[2:]:
+        copy.wait()
     pl.semaphore_wait(barrier, n_ref - 1 + n_dp - 1)
 
     def gather(k):
@@ -172,14 +181,8 @@
     def _(j):
         first(j, other)
         a_copy(j).start()
-
-        @pl.when(j > 0)
-        def _():
-            finish_a(j - 1)
-
         first(j, core)
-
-    finish_a(nj - 1)
+        finish_a(j)
 
     @pl.loop(0, ref_n // BLOCK)
     def _(i):
@@ -316,7 +319,7 @@
     packed = pl.pallas_call(
         functools.partial(kernel, n_dp, n_ref),
         out_shape=jax.ShapeDtypeStruct((rows, 128), F32),
-        in_specs=[vm, vm, vm, pl.BlockSpec(memory_space=pl.ANY), vm, vm],
+        in_specs=[pl.BlockSpec(memory_space=pl.ANY)] * 6,
         out_specs=vm,
         scratch_shapes=[
             V((nj, obs_n, CHUNK), F32), V((nj, obs_n, 2 * CHUNK), BF16),
@@ -328,6 +331,7 @@
             V((obs_n, q), F32),
             V((n_ref, rows, 128), F32), V((n_ref - 1, rows, 128), F32), V((rows, 128), F32), V((n_dp, rows, 128), F32),
             V((2 * feat + 16, q), F32), V((half, 2 * feat + 16), F32), V((half, CHUNK), F32),
+            V((own, feat), F32), V((feat, obs_n), F32), V((feat, ref_n), F32), V((1, ref_n), F32), V((1, feat), F32), dma((5,)),
             dma((nj,)), dma((n_ref,)), dma((n_ref,)), dma((nj,)), dma((nj,)),
             dma((nj, nx)), dma((nj, nx)), dma((nj,)), dma((nj,)),
             dma((n_ref,)), dma((n_ref,)), dma((n_dp,)), dma((n_dp,)),

time: 53.6 us -> 52.6 us (0.981)
  Pallas kernels: 52.7 us -> 51.7 us
    pallas_call x1, Pallas kernels: 51.3 us -> 50.3 us  [body(): pl.pallas_call(functools.partial(kernel, n_dp, n_ref), out_shape=jax.Shap...]
where the time goes in v1:
time: 52.6 us; the launch traced here: 52.3 us
  Pallas kernels  51.7 us (98%)
  between operations  0.64 us (1%)
    pallas_call x1, Pallas kernels, body(): pl.pallas_call(functools.partial(kernel, n_dp, n_ref), out_shape=jax.Shap...  50.3 us
    pallas_call x1, Pallas kernels, body(): pl.pallas_call(functools.partial(finish, ref_n * n_ref), out_shape=(jax.S...  1.4 us

profile of v1, /device:TPU:0, one launch (start us, length us, event | category | flops | bytes accessed | tf_op | source)
XLA Modules:
  0.0 52.3 jit_solution(16752464624555295036)
XLA Ops:
  0.6 50.3 %variance_grad.1.packed_ref = f32[32,128]{1,0:T(8,128)} custom-call(f32[48,64]{1,0:T(8,128)} %cand_hbm.1, f32[64,2048]{1,0:T(8,128)} %bitcast.5, f32[64,1024]{1,0:T(8,128)} %bitcast.6, f32[2048,1024]{1,0:T(8,128)} %slab_ref.1, f32[1,1024]{1,0:T(1,128)} %bitcast.7, f32[1,64]{1,0:T(1,128)} %bitcast.8), custom_call_target="tpu_custom_call" | custom-call | tf_op jit(solution)/shard_map/variance_grad/pallas_call | solution.py:319
  50.9 1.4 %scale_out.1 = (f32[48,64]{1,0:T(8,128)}, f32[1,48]{1,0:T(1,128)}) custom-call(f32[32,128]{1,0:T(8,128)} %variance_grad.1.packed_ref, f32[1,64]{1,0:T(1,128)} %bitcast.9), custom_call_target="tpu_custom_call" | custom-call | tf_op jit(solution)/shard_map/scale_out/pallas_call | solution.py:343

commit v2 on v1

--- a/solution.py
+++ b/solution.py
@@ -11,6 +11,7 @@
 MESH = pl.DeviceIdType.MESH
 CHUNK = 256
 BLOCK = 256
+KBLOCK = 1024
 ROWS = 1024
 NT = (((1,), (1,)), ((), ()))
 VMEM_BYTES = 60 * 1024 * 1024
@@ -139,18 +140,18 @@
     amat[:, 2 * feat:4 * feat] = lo
 
     def kvals(start):
-        rows = pl.ds(pl.multiple_of(start, BLOCK), BLOCK)
+        rows = pl.ds(pl.multiple_of(start, KBLOCK), KBLOCK)
         cross = mm(amat[...], bmat[:, rows])
         return jnp.exp(-0.5 * (unorm[...] + vnorm[:, rows] - 2.0 * cross))
 
-    @pl.loop(0, obs_n // BLOCK)
+    @pl.loop(0, obs_n // KBLOCK)
     def _(i):
-        cols = pl.ds(pl.multiple_of(i * BLOCK, BLOCK), BLOCK)
-        kk = kvals(i * BLOCK)
+        cols = pl.ds(pl.multiple_of(i * KBLOCK, KBLOCK), KBLOCK)
+        kk = kvals(i * KBLOCK)
         kf[:, cols] = kk
         khi, klo = split(kk)
-        k2[:, 0:half, cols] = khi.reshape(2, half, BLOCK)
-        k2[:, half:q, cols] = klo.reshape(2, half, BLOCK)
+        k2[:, 0:half, cols] = khi.reshape(2, half, KBLOCK)
+        k2[:, half:q, cols] = klo.reshape(2, half, KBLOCK)
 
     def a_copy(j):
         return pltpu.make_async_remote_copy(
@@ -184,10 +185,10 @@
         first(j, core)
         finish_a(j)
 
-    @pl.loop(0, ref_n // BLOCK)
+    @pl.loop(0, ref_n // KBLOCK)
     def _(i):
-        cols = pl.ds(pl.multiple_of(i * BLOCK, BLOCK), BLOCK)
-        kref[:, :, cols] = kvals(obs_n + i * BLOCK).reshape(2, half, BLOCK)
+        cols = pl.ds(pl.multiple_of(i * KBLOCK, KBLOCK), KBLOCK)
+        kref[:, :, cols] = kvals(obs_n + i * KBLOCK).reshape(2, half, KBLOCK)
 
     @pl.loop(0, obs_n // BLOCK)
     def _(i):
@@ -219,6 +220,22 @@
                 bhi, blo = split(back)
                 pts = o2[:, rows]
                 gt[...] += mm(pts, bhi) + mm(pts, blo)
+
+    hslots = n_ref // 2
+    rest = own - left
+
+    def combine(g, cands):
+        return g[:, 0:feat] + g[:, feat:2 * feat] - cands * g[:, 2 * feat:2 * feat + 1]
+
+    def stage_direct():
+        mask = (xi == 0).astype(F32)
+        extra = combine(dgrad[...], cand_all[pl.ds(core * hslots, hslots)].reshape(half, feat)) * mask
+        loss = jnp.sum(dloss[...].T, axis=0, keepdims=True) * mask
+        for i in range(hslots):
+            at, slot = i * own, core * hslots + i
+            gout[slot, 0:left, 0:feat] = extra[at:at + left]
+            gout[slot, 0:rest, feat:2 * feat] = extra[at + left:at + own]
+            gout[slot, left:left + 1, 0:own] = loss[:, at:at + own]
 
     for j in range(nj):
         cols = slice(j * CHUNK, (j + 1) * CHUNK)
@@ -244,26 +261,14 @@
             dloss[...] += dl
         if j > 0:
             second(j - 1)
+    stage_direct()
     second(nj - 1)
 
-    def combine(g, cands):
-        return g[:, 0:feat] + g[:, feat:2 * feat] - cands * g[:, 2 * feat:2 * feat + 1]
-
     grad = combine(gt[...].T, cand_all[...].reshape(q, feat))
-    hslots = n_ref // 2
-    mask = (xi == 0).astype(F32)
-    extra = combine(dgrad[...], cand_all[pl.ds(core * hslots, hslots)].reshape(half, feat)) * mask
-    loss = jnp.sum(dloss[...].T, axis=0, keepdims=True) * mask
-    rest = own - left
     for i in range(n_ref):
         at = i * own
-        gout[i, 0:left, 0:feat] = grad[at:at + left]
-        gout[i, 0:rest, feat:2 * feat] = grad[at + left:at + own]
-    for i in range(hslots):
-        at, slot = i * own, core * hslots + i
-        gout[slot, 0:left, 0:feat] += extra[at:at + left]
-        gout[slot, 0:rest, feat:2 * feat] += extra[at + left:at + own]
-        gout[slot, left:left + 1, 0:own] = loss[:, at:at + own]
+        gout[i, 0:left, 0:feat] += grad[at:at + left]
+        gout[i, 0:rest, feat:2 * feat] += grad[at + left:at + own]
 
     def r_copy(k):
         return pltpu.make_async_remote_copy(

time: 52.6 us -> 51.7 us (0.983)
  Pallas kernels: 51.7 us -> 50.8 us
    pallas_call x1, Pallas kernels: 50.3 us -> 49.4 us  [body(): pl.pallas_call(functools.partial(kernel, n_dp, n_ref), out_shape=jax.Shap...]
where the time goes in v2:
time: 51.7 us; the launch traced here: 51.5 us
  Pallas kernels  50.8 us (98%)
  between operations  0.64 us (1%)
    pallas_call x1, Pallas kernels, body(): pl.pallas_call(functools.partial(kernel, n_dp, n_ref), out_shape=jax.Shap...  49.4 us
    pallas_call x1, Pallas kernels, body(): pl.pallas_call(functools.partial(finish, ref_n * n_ref), out_shape=(jax.S...  1.4 us

profile of v2, /device:TPU:0, one launch (start us, length us, event | category | flops | bytes accessed | tf_op | source)
XLA Modules:
  0.0 51.5 jit_solution(5331877250270726702)
XLA Ops:
  0.6 49.4 %variance_grad.1.packed_ref = f32[32,128]{1,0:T(8,128)} custom-call(f32[48,64]{1,0:T(8,128)} %cand_hbm.1, f32[64,2048]{1,0:T(8,128)} %bitcast.5, f32[64,1024]{1,0:T(8,128)} %bitcast.6, f32[2048,1024]{1,0:T(8,128)} %slab_ref.1, f32[1,1024]{1,0:T(1,128)} %bitcast.7, f32[1,64]{1,0:T(1,128)} %bitcast.8), custom_call_target="tpu_custom_call" | custom-call | tf_op jit(solution)/shard_map/variance_grad/pallas_call | solution.py:324
  50.1 1.4 %scale_out.1 = (f32[48,64]{1,0:T(8,128)}, f32[1,48]{1,0:T(1,128)}) custom-call(f32[32,128]{1,0:T(8,128)} %variance_grad.1.packed_ref, f32[1,64]{1,0:T(1,128)} %bitcast.9), custom_call_target="tpu_custom_call" | custom-call | tf_op jit(solution)/shard_map/scale_out/pallas_call | solution.py:348

commit v3 on v2

--- a/solution.py
+++ b/solution.py
@@ -12,7 +12,7 @@
 CHUNK = 256
 BLOCK = 256
 KBLOCK = 1024
-ROWS = 1024
+HEAD_ROWS = 1024
 NT = (((1,), (1,)), ((), ()))
 VMEM_BYTES = 60 * 1024 * 1024
 
@@ -42,7 +42,7 @@
 def kernel(n_dp, n_ref,
            cand_hbm, obs_hbm, refp_hbm, slab_ref, rw_hbm, inv_hbm,
            packed_ref,
-           stage, s2, k2, kf, kt, kref, bmat, vnorm, o2, amat, unorm, cand_all,
+           stage, s_hi, s_lo, w_t, k2, kf, kt, kref, bmat, vnorm, o2, amat, unorm, cand_all,
            pbuf, a_recv, b_buf, b_recv, w_buf, w_recv, acc,
            gout, r_recv, d_send_buf, d_recv_buf, gt, dgrad, dloss,
            cand_ref, obs_ref, refp_ref, rw_ref, inv_ref, in_sem,
@@ -103,12 +103,14 @@
     prep(obs_ref, 0, obs_n)
 
     def split_slab(j):
+        cols = pl.ds(pl.multiple_of(j * CHUNK, CHUNK), CHUNK)
+
         @pl.loop(0, obs_n // BLOCK)
         def _(i):
             rows = pl.ds(pl.multiple_of(i * BLOCK, BLOCK), BLOCK)
             hi, lo = split(stage[j, rows, :])
-            s2[j, rows, 0:CHUNK] = hi
-            s2[j, rows, CHUNK:2 * CHUNK] = lo
+            s_hi[rows, cols] = hi
+            s_lo[rows, cols] = lo
 
     for copy in inputs[2:]:
         copy.wait()
@@ -150,8 +152,8 @@
         kk = kvals(i * KBLOCK)
         kf[:, cols] = kk
         khi, klo = split(kk)
-        k2[:, 0:half, cols] = khi.reshape(2, half, KBLOCK)
-        k2[:, half:q, cols] = klo.reshape(2, half, KBLOCK)
+        k2[0:q, cols] = khi
+        k2[q:2 * q, cols] = klo
 
     def a_copy(j):
         return pltpu.make_async_remote_copy(
@@ -174,16 +176,22 @@
         for m in range(1, nx):
             b_copy(j, m).start()
 
-    def first(j, h):
-        x = mm(k2[h], s2[j, :, 0:CHUNK])
-        pbuf[j, h] = x[0:half] + x[half:q] + mm(k2[h, 0:half, :], s2[j, :, CHUNK:2 * CHUNK])
+    def first(j):
+        cols = pl.ds(pl.multiple_of(j * CHUNK, CHUNK), CHUNK)
+        x = mm(k2[...], s_hi[:, cols])
+        x = x[0:q] + x[q:2 * q] + mm(k2[0:q, :], s_lo[:, cols])
+        pbuf[j] = x.reshape(2, half, CHUNK)
 
     @pl.loop(0, nj)
     def _(j):
-        first(j, other)
+        first(j)
         a_copy(j).start()
-        first(j, core)
-        finish_a(j)
+
+        @pl.when(j > 0)
+        def _():
+            finish_a(j - 1)
+
+    finish_a(nj - 1)
 
     @pl.loop(0, ref_n // KBLOCK)
     def _(i):
@@ -195,31 +203,39 @@
         rows = pl.ds(pl.multiple_of(i * BLOCK, BLOCK), BLOCK)
         kt[rows, :] = kf[:, rows].T
 
-    gt[...] = jnp.zeros_like(gt)
     gout[...] = jnp.zeros_like(gout)
 
-    def second(j):
+    def place(j):
         c_copy(j).wait()
         w, wr = w_buf[j], w_recv[j]
         low = core == 0
         wt = jnp.concatenate([jnp.where(low, w, wr), jnp.where(low, wr, w)], axis=0).T
         whi, wlo = split(wt)
-        whl = jnp.concatenate([whi, wlo], axis=1)
-
-        @pl.loop(0, obs_n // ROWS)
+        w_t[j * CHUNK:(j + 1) * CHUNK, 0:q] = whi
+        w_t[j * CHUNK:(j + 1) * CHUNK, q:2 * q] = wlo
+
+    head = max(nj - 2, 0) * CHUNK
+
+    def second(rows, k0, k1):
+        x = mm(s_hi[rows, k0:k1], w_t[k0:k1, :])
+        return x[:, 0:q] + x[:, q:2 * q] + mm(s_lo[rows, k0:k1], w_t[k0:k1, 0:q])
+
+    def second_head(j):
+        @pl.loop(0, obs_n // HEAD_ROWS)
         def _(i):
-            rows = pl.ds(pl.multiple_of(i * ROWS, ROWS), ROWS)
-            x = mm(s2[j, rows, 0:CHUNK], whl)
-            prod = x[:, 0:q] + x[:, q:2 * q] + mm(s2[j, rows, CHUNK:2 * CHUNK], whi)
+            rows = pl.ds(pl.multiple_of(i * HEAD_ROWS, HEAD_ROWS), HEAD_ROWS)
+            prod = second(rows, j * CHUNK, (j + 1) * CHUNK)
             if j > 0:
                 prod = acc[rows, :] + prod
-            if j < nj - 1:
-                acc[rows, :] = prod
-            else:
-                back = -prod * kt[rows, :]
-                bhi, blo = split(back)
-                pts = o2[:, rows]
-                gt[...] += mm(pts, bhi) + mm(pts, blo)
+            acc[rows, :] = prod
+
+    def second_last():
+        prod = second(slice(0, obs_n), head, ref_n)
+        if head > 0:
+            prod = acc[...] + prod
+        bhi, blo = split(-prod * kt[...])
+        pts = o2[:, 0:obs_n]
+        gt[...] = mm(pts, bhi) + mm(pts, blo)
 
     hslots = n_ref // 2
     rest = own - left
@@ -260,9 +276,12 @@
             dgrad[...] += dg
             dloss[...] += dl
         if j > 0:
-            second(j - 1)
+            place(j - 1)
+            if j < nj - 1:
+                second_head(j - 1)
     stage_direct()
-    second(nj - 1)
+    place(nj - 1)
+    second_last()
 
     grad = combine(gt[...].T, cand_all[...].reshape(q, feat))
     for i in range(n_ref):
@@ -327,8 +346,8 @@
         in_specs=[pl.BlockSpec(memory_space=pl.ANY)] * 6,
         out_specs=vm,
         scratch_shapes=[
-            V((nj, obs_n, CHUNK), F32), V((nj, obs_n, 2 * CHUNK), BF16),
-            V((2, q, obs_n), BF16), V((q, obs_n), F32), V((obs_n, q), F32), V((2, half, ref_n), F32),
+            V((nj, obs_n, CHUNK), F32), V((obs_n, ref_n), BF16), V((obs_n, ref_n), BF16), V((ref_n, 2 * q), BF16),
+            V((2 * q, obs_n), BF16), V((q, obs_n), F32), V((obs_n, q), F32), V((2, half, ref_n), F32),
             V((4 * feat, obs_n + ref_n), BF16), V((1, obs_n + ref_n), F32), V((2 * feat + 16, obs_n + ref_n), BF16),
             V((q, 4 * feat), BF16), V((q, 1), F32), V((n_ref, own, feat), F32),
             V((nj, 2, half, CHUNK), F32), V((nj, half, CHUNK), F32), V((nj, half, CHUNK), F32),

time: 51.7 us -> 51.3 us (level)
  no operation moved by 1% of the time
where the time goes in v3:
time: 51.3 us; the launch traced here: 51 us
  Pallas kernels  50.3 us (98%)
  between operations  0.64 us (1%)
    pallas_call x1, Pallas kernels, body(): pl.pallas_call(functools.partial(kernel, n_dp, n_ref), out_shape=jax.Shap...  48.9 us
    pallas_call x1, Pallas kernels, body(): pl.pallas_call(functools.partial(finish, ref_n * n_ref), out_shape=(jax.S...  1.4 us

profile of v3, /device:TPU:0, one launch (start us, length us, event | category | flops | bytes accessed | tf_op | source)
XLA Modules:
  0.0 51.0 jit_solution(12150538858320979763)
XLA Ops:
  0.6 48.9 %variance_grad.1.packed_ref = f32[32,128]{1,0:T(8,128)} custom-call(f32[48,64]{1,0:T(8,128)} %cand_hbm.1, f32[64,2048]{1,0:T(8,128)} %bitcast.5, f32[64,1024]{1,0:T(8,128)} %bitcast.6, f32[2048,1024]{1,0:T(8,128)} %slab_ref.1, f32[1,1024]{1,0:T(1,128)} %bitcast.7, f32[1,64]{1,0:T(1,128)} %bitcast.8), custom_call_target="tpu_custom_call" | custom-call | tf_op jit(solution)/shard_map/variance_grad/pallas_call | solution.py:343
  49.6 1.4 %scale_out.1 = (f32[48,64]{1,0:T(8,128)}, f32[1,48]{1,0:T(1,128)}) custom-call(f32[32,128]{1,0:T(8,128)} %variance_grad.1.packed_ref, f32[1,64]{1,0:T(1,128)} %bitcast.9), custom_call_target="tpu_custom_call" | custom-call | tf_op jit(solution)/shard_map/scale_out/pallas_call | solution.py:367
